TPU v7x, 32 devices: a whole 2x2x4 slice. The times are simulated.
32 devices in a mesh: dp: 8 (over z, y), tensor: 4 (over x, core).
Axes of the slice: x: 2, y: 2, z: 4, core: 2. Of those that a mesh axis runs over, the one named last changes fastest.
Arguments:
- tokens: bfloat16 [16384, 768], P(('dp', 'tensor')), may hold values from -12 to 12
- grad_out: bfloat16 [16384, 768], P(('dp', 'tensor')), may hold values from -6 to 6
- lengths: int32 [32], P('dp'), may hold values from 204 to 512, as said below
- segment_ids: int32 [32, 512], P('dp'), may hold values from 0 to 3, never falling along the last dimension, each value on 1 to 256 neighbouring positions
- query_weight: bfloat16 [768, 768], P(None, 'tensor'), may hold values from -0.21875 to 0.21875
- query_bias: bfloat16 [768], P('tensor'), may hold values from -3 to 3
- key_weight: bfloat16 [768, 768], P(None, 'tensor'), may hold values from -0.21875 to 0.21875
- value_weight: bfloat16 [768, 768], P(None, 'tensor'), may hold values from -0.21875 to 0.21875
- value_bias: bfloat16 [768], P('tensor'), may hold values from -3 to 3
- mixer_weight: bfloat16 [768, 768], P('tensor'), may hold values from -0.625 to 0.625
- mixer_bias: bfloat16 [768], replicated, may hold values from -3 to 3
- first_gain: bfloat16 [768], replicated, may hold values from 0.5 to 1.5
- first_shift: bfloat16 [768], replicated, may hold values from -2 to 2
- inner_weight: bfloat16 [768, 3072], P(None, 'tensor'), may hold values from -0.21875 to 0.21875
- inner_bias: bfloat16 [3072], P('tensor'), may hold values from -3 to 3
- outer_weight: bfloat16 [3072, 768], P('tensor'), may hold values from -0.109375 to 0.109375
- outer_bias: bfloat16 [768], replicated, may hold values from -2 to 2
- second_gain: bfloat16 [768], replicated, may hold values from 0.5 to 1.5
- second_shift: bfloat16 [768], replicated, may hold values from -2 to 2
Outputs:
- layer_out: bfloat16 [16384, 768], P(('dp', 'tensor'))
- tokens_grad: float32 [16384, 768], P(('dp', 'tensor'))
- query_weight_grad: float32 [768, 768], P(None, 'tensor')
- query_bias_grad: float32 [768], P('tensor')
- key_weight_grad: float32 [768, 768], P(None, 'tensor')
- value_weight_grad: float32 [768, 768], P(None, 'tensor')
- value_bias_grad: float32 [768], P('tensor')
- mixer_weight_grad: float32 [768, 768], P('tensor')
- mixer_bias_grad: float32 [768], replicated
- first_gain_grad: float32 [768], replicated
- first_shift_grad: float32 [768], replicated
- inner_weight_grad: float32 [768, 3072], P(None, 'tensor')
- inner_bias_grad: float32 [3072], P('tensor')
- outer_weight_grad: float32 [3072, 768], P('tensor')
- outer_bias_grad: float32 [768], replicated
- second_gain_grad: float32 [768], replicated
- second_shift_grad: float32 [768], replicated
- statistics: float32 [3], replicated
Inputs may be any that keep to these rules, and one draw needn't show every extreme that they name: `lengths`: the first sequence holds (1024) // 5 tokens and the last is full. `segment_ids`: never fall along a sequence; a segment holds at most 256 rows.
All inputs are finite; a program needn't handle non-finite values.
Results may differ from a plain program's by a relative error of at most 0.018.
Values may be sent and summed in bfloat16 or wider, within the bound.
No kernel may reach another device: no remote copies, remote signals or barrier semaphores. Data moves between devices by JAX's collectives and lax.ppermute only.
A program may use at most 128 MiB of HBM per device.

v0:
```python
import jax
import jax.numpy as jnp
from jax import lax
from jax.sharding import PartitionSpec as P

D = 768
HEAD_DIM = 64
L = 512


eps_norm = 1e-06
root_half = 0.7071067811865476
inv_root_tau = 0.3989422804014327


def layer_norm(token_rows, norm_gain, norm_shift):
    center = token_rows - jnp.mean(token_rows, axis=-1, keepdims=True)
    inverse = lax.rsqrt(jnp.mean(center * center, axis=-1, keepdims=True) + eps_norm)
    normed = center * inverse
    return (normed * norm_gain + norm_shift, normed, inverse)


def norm_backward(incoming, normed, inverse, norm_gain):
    scaled = incoming * norm_gain
    middle = jnp.mean(scaled, axis=-1, keepdims=True)
    along = jnp.mean(scaled * normed, axis=-1, keepdims=True)
    return inverse * (scaled - middle - normed * along)


def gelu_slope(inner_pre):
    return (
        0.5 * (1.0 + lax.erf(inner_pre * root_half))
        + inner_pre * jnp.exp(-0.5 * inner_pre * inner_pre) * inv_root_tau
    )


def allowed_pairs(segment_row, seq_length):
    position = jnp.arange(L, dtype=jnp.int32)
    same_doc = segment_row[:, None] == segment_row[None, :]
    live_key = position[None, :] < seq_length
    return same_doc & live_key | (position[:, None] == position[None, :])


def masked_scores(queries, key_rows, segment_row, seq_length):
    raw_scores = jnp.einsum("qhd,khd->hqk", queries, key_rows, preferred_element_type=jnp.float32)
    return jnp.where(
        allowed_pairs(segment_row, seq_length)[None], raw_scores * float(HEAD_DIM) ** (-0.5), -1e30
    )


def attend_forward(packed):
    queries, key_rows, values, segment_row, seq_length = packed
    scores = masked_scores(queries, key_rows, segment_row, seq_length)
    highest = jnp.max(scores, axis=-1, keepdims=True)
    expanded = jnp.exp(scores - highest)
    row_total = jnp.sum(expanded, axis=-1, keepdims=True)
    softmax_low = (expanded / row_total).astype(jnp.bfloat16)
    attended = jnp.einsum("hqk,khd->qhd", softmax_low, values, preferred_element_type=jnp.float32)
    return (attended.astype(jnp.bfloat16), (highest + jnp.log(row_total))[..., 0])


def attend_backward(packed):
    queries, key_rows, values, attended_grad, log_total, segment_row, seq_length = packed
    scores = masked_scores(queries, key_rows, segment_row, seq_length)
    softmax_out = jnp.exp(scores - log_total[..., None])
    probs_grad = jnp.einsum(
        "qhd,khd->hqk", attended_grad, values, preferred_element_type=jnp.float32
    )
    row_dot = jnp.sum(softmax_out * probs_grad, axis=-1, keepdims=True)
    scores_grad = (softmax_out * (probs_grad - row_dot) * float(HEAD_DIM) ** (-0.5)).astype(
        jnp.bfloat16
    )
    queries_grad = jnp.einsum(
        "hqk,khd->qhd", scores_grad, key_rows, preferred_element_type=jnp.float32
    )
    keys_grad = jnp.einsum("hqk,qhd->khd", scores_grad, queries, preferred_element_type=jnp.float32)
    values_grad = jnp.einsum(
        "hqk,qhd->khd",
        softmax_out.astype(jnp.bfloat16),
        attended_grad,
        preferred_element_type=jnp.float32,
    )
    return (queries_grad, keys_grad, values_grad)


def body(
    tokens,
    grad_out,
    lengths,
    segment_ids,
    query_weight,
    query_bias,
    key_weight,
    value_weight,
    value_bias,
    mixer_weight,
    mixer_bias,
    first_gain,
    first_shift,
    inner_weight,
    inner_bias,
    outer_weight,
    outer_bias,
    second_gain,
    second_shift,
):
    width_here = query_weight.shape[1]
    heads_here = width_here // HEAD_DIM
    own_rows = tokens.shape[0]
    seq_here = segment_ids.shape[0]
    group_rows = seq_here * L
    head_shape = (seq_here, L, heads_here, HEAD_DIM)
    united_weight = jnp.concatenate([query_weight, key_weight, value_weight], axis=1)
    gathered = lax.all_gather(tokens, "tensor", axis=0, tiled=True)
    united = jnp.dot(gathered, united_weight, preferred_element_type=jnp.float32)
    queries = (united[:, :width_here] + query_bias).astype(jnp.bfloat16)
    key_rows = united[:, width_here : 2 * width_here].astype(jnp.bfloat16)
    values = (united[:, 2 * width_here :] + value_bias).astype(jnp.bfloat16)
    queries = queries.reshape(head_shape)
    key_rows = key_rows.reshape(head_shape)
    values = values.reshape(head_shape)
    attended, log_total = lax.map(attend_forward, (queries, key_rows, values, segment_ids, lengths))
    attended = attended.reshape(group_rows, width_here)
    attn_branch = (
        lax.psum_scatter(
            jnp.dot(attended, mixer_weight, preferred_element_type=jnp.float32),
            "tensor",
            scatter_dimension=0,
            tiled=True,
        )
        + mixer_bias
    )
    token_float = tokens.astype(jnp.float32)
    normed_one, first_hat, first_inverse = layer_norm(
        token_float + attn_branch, first_gain, first_shift
    )
    normed_low = normed_one.astype(jnp.bfloat16)
    normed_all = lax.all_gather(normed_low, "tensor", axis=0, tiled=True)
    inner_pre = jnp.dot(normed_all, inner_weight, preferred_element_type=jnp.float32) + inner_bias
    activated = jax.nn.gelu(inner_pre, approximate=False).astype(jnp.bfloat16)
    ffn_branch = (
        lax.psum_scatter(
            jnp.dot(activated, outer_weight, preferred_element_type=jnp.float32).astype(
                jnp.bfloat16
            ),
            "tensor",
            scatter_dimension=0,
            tiled=True,
        ).astype(jnp.float32)
        + outer_bias
    )
    layer_out, second_hat, second_inverse = layer_norm(
        normed_one + ffn_branch, second_gain, second_shift
    )
    row_index = lax.axis_index("tensor") * own_rows + jnp.arange(own_rows, dtype=jnp.int32)
    owner = (row_index // L)[:, None] == jnp.arange(seq_here, dtype=jnp.int32)[None, :]
    row_length = jnp.sum(jnp.where(owner, lengths[None, :], 0), axis=1)
    valid_rows = (row_index % L < row_length).astype(jnp.float32)
    stat_terms = jnp.stack(
        [
            jnp.sum(valid_rows * jnp.sum(token_float * token_float, axis=-1)),
            jnp.sum(valid_rows * jnp.sum(attn_branch * attn_branch, axis=-1)),
            jnp.sum(valid_rows * jnp.sum(ffn_branch * ffn_branch, axis=-1)),
        ]
    )
    valid_count = jnp.sum(valid_rows)
    stat_totals, count_total = lax.psum((stat_terms, valid_count), ("dp", "tensor"))
    incoming = grad_out.astype(jnp.float32)
    second_gain_grad = jnp.sum(incoming * second_hat, axis=0)
    second_shift_grad = jnp.sum(incoming, axis=0)
    second_grad = norm_backward(incoming, second_hat, second_inverse, second_gain)
    outer_bias_grad = jnp.sum(second_grad, axis=0)
    ffn_all = lax.all_gather(second_grad.astype(jnp.bfloat16), "tensor", axis=0, tiled=True)
    outer_weight_grad = jnp.einsum(
        "gf,gd->fd", activated, ffn_all, preferred_element_type=jnp.float32
    )
    inner_grad = jnp.einsum(
        "gd,fd->gf", ffn_all, outer_weight, preferred_element_type=jnp.float32
    ) * gelu_slope(inner_pre)
    inner_bias_grad = jnp.sum(inner_grad, axis=0)
    inner_low = inner_grad.astype(jnp.bfloat16)
    inner_weight_grad = jnp.einsum(
        "gd,gf->df", normed_all, inner_low, preferred_element_type=jnp.float32
    )
    normed_grad = second_grad + lax.psum_scatter(
        jnp.einsum("gf,df->gd", inner_low, inner_weight, preferred_element_type=jnp.float32).astype(
            jnp.bfloat16
        ),
        "tensor",
        scatter_dimension=0,
        tiled=True,
    ).astype(jnp.float32)
    first_gain_grad = jnp.sum(normed_grad * first_hat, axis=0)
    first_shift_grad = jnp.sum(normed_grad, axis=0)
    first_grad = norm_backward(normed_grad, first_hat, first_inverse, first_gain)
    mixer_bias_grad = jnp.sum(first_grad, axis=0)
    branch_all = lax.all_gather(first_grad.astype(jnp.bfloat16), "tensor", axis=0, tiled=True)
    mixer_weight_grad = jnp.einsum(
        "gc,gd->cd", attended, branch_all, preferred_element_type=jnp.float32
    )
    attended_grad = jnp.einsum(
        "gd,cd->gc", branch_all, mixer_weight, preferred_element_type=jnp.float32
    ).astype(jnp.bfloat16)
    queries_grad, keys_grad, values_grad = lax.map(
        attend_backward,
        (
            queries,
            key_rows,
            values,
            attended_grad.reshape(head_shape),
            log_total,
            segment_ids,
            lengths,
        ),
    )
    queries_grad = queries_grad.reshape(group_rows, width_here)
    keys_grad = keys_grad.reshape(group_rows, width_here)
    values_grad = values_grad.reshape(group_rows, width_here)
    query_bias_grad = jnp.sum(queries_grad, axis=0)
    value_bias_grad = jnp.sum(values_grad, axis=0)
    united_low = jnp.concatenate(
        [
            queries_grad.astype(jnp.bfloat16),
            keys_grad.astype(jnp.bfloat16),
            values_grad.astype(jnp.bfloat16),
        ],
        axis=1,
    )
    united_grad = jnp.einsum("gd,gc->dc", gathered, united_low, preferred_element_type=jnp.float32)
    query_weight_grad = united_grad[:, :width_here]
    key_weight_grad = united_grad[:, width_here : 2 * width_here]
    value_weight_grad = united_grad[:, 2 * width_here :]
    tokens_grad = first_grad + lax.psum_scatter(
        jnp.einsum(
            "gc,dc->gd", united_low, united_weight, preferred_element_type=jnp.float32
        ).astype(jnp.bfloat16),
        "tensor",
        scatter_dimension=0,
        tiled=True,
    ).astype(jnp.float32)
    (
        query_weight_grad,
        key_weight_grad,
        value_weight_grad,
        query_bias_grad,
        value_bias_grad,
        mixer_weight_grad,
        inner_weight_grad,
        inner_bias_grad,
        outer_weight_grad,
    ) = lax.psum(
        (
            query_weight_grad,
            key_weight_grad,
            value_weight_grad,
            query_bias_grad,
            value_bias_grad,
            mixer_weight_grad,
            inner_weight_grad,
            inner_bias_grad,
            outer_weight_grad,
        ),
        "dp",
    )
    (
        mixer_bias_grad,
        first_gain_grad,
        first_shift_grad,
        outer_bias_grad,
        second_gain_grad,
        second_shift_grad,
    ) = lax.psum(
        (
            mixer_bias_grad,
            first_gain_grad,
            first_shift_grad,
            outer_bias_grad,
            second_gain_grad,
            second_shift_grad,
        ),
        ("dp", "tensor"),
    )
    statistics = jnp.sqrt(stat_totals / (count_total * D))
    return (
        layer_out.astype(jnp.bfloat16),
        tokens_grad,
        query_weight_grad,
        query_bias_grad,
        key_weight_grad,
        value_weight_grad,
        value_bias_grad,
        mixer_weight_grad,
        mixer_bias_grad,
        first_gain_grad,
        first_shift_grad,
        inner_weight_grad,
        inner_bias_grad,
        outer_weight_grad,
        outer_bias_grad,
        second_gain_grad,
        second_shift_grad,
        statistics,
    )


def solution(mesh):
    in_specs = (
        P(("dp", "tensor"), None),
        P(("dp", "tensor"), None),
        P("dp"),
        P("dp", None),
        P(None, "tensor"),
        P("tensor"),
        P(None, "tensor"),
        P(None, "tensor"),
        P("tensor"),
        P("tensor", None),
        P(),
        P(),
        P(),
        P(None, "tensor"),
        P("tensor"),
        P("tensor", None),
        P(),
        P(),
        P(),
    )
    out_specs = (
        P(("dp", "tensor"), None),
        P(("dp", "tensor"), None),
        P(None, "tensor"),
        P("tensor"),
        P(None, "tensor"),
        P(None, "tensor"),
        P("tensor"),
        P("tensor", None),
        P(),
        P(),
        P(),
        P(None, "tensor"),
        P("tensor"),
        P("tensor", None),
        P(),
        P(),
        P(),
        P(),
    )
    return jax.shard_map(body, mesh=mesh, in_specs=in_specs, out_specs=out_specs, check_vma=False)
```

profile of v0, /device:TPU:16, one launch (start us, length us, event | category | flops | bytes accessed | tf_op | source)
XLA Modules:
  0.0 766.7 jit_solution(1244130350556778765)
XLA Ops:
  12.3 26.9 %all-gather.5.cloned.1.call-done = bf16[2048,768]{1,0:T(8,128)(2,1)} async-done(((bf16[512,768]{1,0:T(8,128)(2,1)}), bf16[2048,768]{1,0:T(8,128)(2,1)}) %all-gather.5.cloned.1.call-update) | async-done | bytes 3145744 | tf_op jit(solution)/shard_map/all_gather | solution.py:114
  39.2 3.9 convolution_bitcast_fusion
  45.8 3.0 reshape.282
  50.1 24.3 %while.26 = (s32[]{:T(128)}, bf16[4,512,3,64]{1,3,2,0:T(8,128)(2,1)}, f32[4,3,512]{2,1,0:T(4,128)}, bf16[4,512,3,64]{1,3,2,0:T(8,128)(2,1)S(1)}, s32[4,512]{1,0:...) while((s32[]{:T(128)}, ...), condition=%wide.region_3.4_spmd, body=%wide.region_0.3_spmd.sunk | while | flops 211909632 | bytes 11336829 | solution.py:122
  53.8 1.8 fusion.171
  59.9 1.8 fusion.171
  66.0 1.8 fusion.171
  72.0 1.8 fusion.171
  74.4 2.4 copy.70
  77.0 3.7 fusion.120
  81.4 57.9 %reduce-scatter.5.cloned.1.call-done = f32[512,768]{1,0:T(8,128)} async-done(((f32[2048,768]{1,0:T(8,128)}), f32[512,768]{1,0:T(8,128)}) %reduce-scatter.5.cloned.1.call-update) | async-done | bytes 1572880 | tf_op jit(solution)/shard_map/reduce_scatter | solution.py:125
  139.3 2.8 fusion.115
  145.1 27.2 %all-gather.7.cloned.1.call-done = bf16[2048,768]{1,0:T(8,128)(2,1)} async-done(((bf16[512,768]{1,0:T(8,128)(2,1)}), bf16[2048,768]{1,0:T(8,128)(2,1)}) %all-gather.7.cloned.1.call-update) | async-done | bytes 3145744 | tf_op jit(solution)/shard_map/all_gather | solution.py:138
  172.3 17.9 %fusion.77 = (bf16[2048,768]{1,0:T(8,128)(2,1)S(1)}, f32[2048,768]{1,0:T(8,128)}) fusion(f32[768]{0:T(1024)} %convert_element_type.126, bf16[2048,768]{1,0:T(8,128)(2,1)} %all-gather.7.cloned.1.call-done, bf16[768,768]{1,0:T(8,128)(2,1)S(1)} %copy-done), kind=kOutput, calls=%fused_computation.75 | convolution fusion | flops 2519728128 | bytes 13765632 | tf_op jit(solution)/shard_map/dot_general | solution.py:139
  190.1 1.7 copy-done.41
  191.8 4.0 convolution_convert_fusion.1
  199.7 34.2 %reduce-scatter.7.cloned.1.call-done = bf16[512,768]{1,0:T(8,128)(2,1)} async-done(((bf16[2048,768]{1,0:T(8,128)(2,1)}), bf16[512,768]{1,0:T(8,128)(2,1)}) %reduce-scatter.7.cloned.1.call-update) | async-done | bytes 786448 | tf_op jit(solution)/shard_map/reduce_scatter | solution.py:142
  233.9 2.5 fusion.113
  238.1 2.3 fusion.111
  240.5 28.6 %all-gather.9.cloned.1.call-done = bf16[2048,768]{1,0:T(8,128)(2,1)} async-done(((bf16[512,768]{1,0:T(8,128)(2,1)}), bf16[2048,768]{1,0:T(8,128)(2,1)}) %all-gather.9.cloned.1.call-update) | async-done | bytes 3145744 | tf_op jit(solution)/shard_map/all_gather | solution.py:173
  269.1 7.5 fusion.119
  276.6 1.7 copy-done.42
  278.3 4.0 convolution_convert_fusion
  282.6 37.9 %reduce-scatter.9.cloned.1.call-done = bf16[512,768]{1,0:T(8,128)(2,1)} async-done(((bf16[2048,768]{1,0:T(8,128)(2,1)}), bf16[512,768]{1,0:T(8,128)(2,1)}) %reduce-scatter.9.cloned.1.call-update) | async-done | bytes 786448 | tf_op jit(solution)/shard_map/reduce_scatter | solution.py:185
  320.5 3.2 multiply_reduce_fusion.3
  327.1 28.6 %all-gather.11.cloned.1.call-done = bf16[2048,768]{1,0:T(8,128)(2,1)} async-done(((bf16[512,768]{1,0:T(8,128)(2,1)}), bf16[2048,768]{1,0:T(8,128)(2,1)}) %all-gather.11.cloned.1.call-update) | async-done | bytes 3145744 | tf_op jit(solution)/shard_map/all_gather | solution.py:197
  355.7 3.0 convolution_convert_fusion.3
  358.7 1.4 reshape.286
  361.5 95.2 %while.27 = (s32[]{:T(128)}, f32[4,512,3,64]{1,3,2,0:T(8,128)}, bf16[4,512,3,64]{1,3,2,0:T(8,128)(2,1)}, f32[4,512,3,64]{1,3,2,0:T(8,128)}, bf16[4,512,3,64]{1,3...) while((s32[]{:T(128)}, f32[4,512,3,64]{1,3,2,0:T(8,128)}, ...), condition=%wide.region_17.18_spmd, body=%wide.region_15.17_spmd.sunk | while | flops 515379712 | bytes 50299056 | solution.py:204
  364.4 1.9 subtract_exponential_fusion.3
  366.3 1.7 copy-done.1
  369.4 3.2 fusion.183
  372.6 6.3 fusion.185
  378.9 6.5 fusion.184
  388.2 1.9 subtract_exponential_fusion.3
  390.1 1.7 copy-done.1
  393.2 3.2 fusion.183
  396.4 6.3 fusion.185
  402.7 6.5 fusion.184
  412.1 1.9 subtract_exponential_fusion.3
  414.0 1.7 copy-done.1
  417.0 3.2 fusion.183
  420.2 6.3 fusion.185
  426.5 6.5 fusion.184
  435.9 1.9 subtract_exponential_fusion.3
  437.8 1.7 copy-done.1
  440.8 3.2 fusion.183
  444.0 6.3 fusion.185
  450.3 6.5 fusion.184
  456.7 3.3 fusion.117
  464.1 4.1 convolution_convert_fusion.2
  468.5 7.1 fusion.122
  475.6 4.1 fusion.100
  479.7 2.0 convolution_bitcast_fusion.1
  484.3 1.6 fusion.121
  487.2 2.0 pad_maximum_fusion
  489.3 40.6 %all-reduce = (f32[768]{0:T(1024)}, f32[768]{0:T(1024)}, f32[768]{0:T(1024)}, f32[768]{0:T(1024)}, f32[768]{0:T(1024)}, /*index=5*/f32[768]{0:T(1024)}, f32[3]{0:T(128)S(1)}, f32[]{:T(128)}) all-reduce(f32[768]{0:T(1024)S(1)} %copy-done.27, f32[768]{0:T(1024)S(1)} %copy-done.24, ...), channel_id=1, replica_groups=mesh['dp'=8,'tensor'=4] {'dp','tensor'}, use_global_device_ids=true, to_apply=%region_28.29 | all-reduce | flops 4612 | bytes 36896 | tf_op jit(solution)/shard_map/psum | solution.py:272
  531.2 19.9 %all-reduce.1 = (f32[192]{0:T(256)}, f32[192]{0:T(256)}, f32[768]{0:T(1024)}) all-reduce(f32[192]{0:T(256)S(1)} %reduce_sum.256, f32[192]{0:T(256)S(1)} %reduce_sum.258, f32[768]{0:T(1024)S(1)} %copy-done.32), channel_id=1, replica_groups=mesh['dp'=8,'tensor'=4] {'dp'}, use_global_device_ids=true, to_apply=%region_21.22 | all-reduce | flops 1152 | bytes 9216 | tf_op jit(solution)/shard_map/psum | solution.py:251
  551.1 2.5 convert_add_fusion.1
  553.6 196.5 %all-reduce.5.cloned.1.call-done = (f32[768,192]{0,1:T(8,128)}, f32[768,192]{0,1:T(8,128)}, f32[768,192]{0,1:T(8,128)}, f32[192,768]{1,0:T(8,128)}, f32[768,768]{1,0:T(8,128)}, /*index=5*/f32[768,768]{1,0:T(8,128)}) async-done(((f32[768,192]{0,1:T(8,128)}, f32[768,192]{0,1:T(8,128)}, f32[768,192]{0,1:T(8,128)}, f32[192,768]{1,0:T(8,128)}, f32[768,768]{1,0:T(8,128)}, /*index=5*/f32[768,768]{1,0:T(8,128)}), ...) | async-done | bytes 7077904 | tf_op jit(solution)/shard_map/psum | solution.py:251
  750.2 2.1 copy.124
  752.2 1.9 copy.125
  754.1 1.9 copy.126
  756.9 1.4 copy.128
  (217 shorter events, 68.5 us)
Async XLA Ops:
  7.2 165.1 %copy-start = (bf16[768,768]{1,0:T(8,128)(2,1)S(1)}, bf16[768,768]{1,0:T(8,128)(2,1)}, u32[]{:S(2)}) copy-start(bf16[768,768]{1,0:T(8,128)(2,1)} %param.36) | copy-start | bytes 3538948
  7.2 32.0 %all-gather.5.cloned.1.call-start = ((), (), s32[]{:S(2)}) async-start(), calls=%async_computation.4 | async-start | bytes 3932160 | tf_op jit(solution)/shard_map/all_gather | solution.py:114
  7.9 131.3 %reduce-scatter.5.cloned.1.call-start = ((), (), s32[]{:S(2)}) async-start(), calls=%async_computation.5 | async-start | bytes 7864320 | tf_op jit(solution)/shard_map/reduce_scatter | solution.py:125
  12.3 27.0 %copy-start.20 = (bf16[768,576]{0,1:T(8,128)(2,1)}, bf16[768,576]{0,1:T(8,128)(2,1)S(1)}, u32[]{:S(2)}) copy-start(bf16[768,576]{0,1:T(8,128)(2,1)S(1)} %constant_dynamic-update-slice_fusion) | copy-start | bytes 2654212
  45.1 5.0 copy-start.36
  74.4 2.4 copy-start.5
  74.4 6.3 copy-start.7
  74.4 6.3 copy-start.8
  74.4 2.6 copy-start.16
  80.7 0.7 copy-start.33
  80.7 0.7 copy-start.34
  80.7 0.7 copy-start.35
  80.7 91.5 %all-gather.7.cloned.1.call-start = ((), (), s32[]{:S(2)}) async-start(), calls=%async_computation.6 | async-start | bytes 3932160 | tf_op jit(solution)/shard_map/all_gather | solution.py:138
  143.6 90.3 %reduce-scatter.7.cloned.1.call-start = ((), (), s32[]{:S(2)}) async-start(), calls=%async_computation.7 | async-start | bytes 3932160 | tf_op jit(solution)/shard_map/reduce_scatter | solution.py:142
  172.3 19.5 %copy-start.40 = (bf16[768,768]{1,0:T(8,128)(2,1)S(1)}, bf16[768,768]{1,0:T(8,128)(2,1)}, u32[]{:S(2)}) copy-start(bf16[768,768]{1,0:T(8,128)(2,1)} %param.38) | copy-start | bytes 3538948
  190.1 1.7 copy-start.41
  195.8 73.3 %all-gather.9.cloned.1.call-start = ((), (), s32[]{:S(2)}) async-start(), calls=%async_computation.8 | async-start | bytes 3932160 | tf_op jit(solution)/shard_map/all_gather | solution.py:173
  233.9 2.8 copy-start.10
  233.9 2.8 copy-start.22
  233.9 4.1 copy-start.28
  240.4 80.1 %reduce-scatter.9.cloned.1.call-start = ((), (), s32[]{:S(2)}) async-start(), calls=%async_computation.9 | async-start | bytes 3932160 | tf_op jit(solution)/shard_map/reduce_scatter | solution.py:185
  276.6 1.7 copy-start.42
  282.3 73.3 %all-gather.11.cloned.1.call-start = ((), (), s32[]{:S(2)}) async-start(), calls=%async_computation.10 | async-start | bytes 3932160 | tf_op jit(solution)/shard_map/all_gather | solution.py:197
  320.5 3.2 copy-start.4
  320.5 3.2 copy-start.11
  324.9 1.1 copy-start.2
  324.9 30.8 %copy-start.17 = (bf16[192,768]{1,0:T(8,128)(2,1)S(1)}, bf16[192,768]{1,0:T(8,128)(2,1)}, u32[]{:S(2)}) copy-start(bf16[192,768]{1,0:T(8,128)(2,1)} %param.32) | copy-start | bytes 884740
  327.0 224.2 %reduce-scatter.11.cloned.1.call-start = ((), (), s32[]{:S(2)}) async-start(), calls=%async_computation.11 | async-start | bytes 3932160 | tf_op jit(solution)/shard_map/reduce_scatter | solution.py:233
  358.7 2.8 copy-start.6
  358.7 2.8 copy-start.37
  366.3 1.7 copy-start.1
  390.1 1.7 copy-start.1
  414.0 1.7 copy-start.1
  437.8 1.7 copy-start.1
  460.0 1.6 copy-start.14
  462.3 1.8 copy-start.21
  462.7 1.4 copy-start.18
  468.2 282.0 %all-reduce.5.cloned.1.call-start = ((), (), s32[]{:S(2)}) async-start(), calls=%async_computation.12 | async-start | bytes 14155776 | tf_op jit(solution)/shard_map/psum | solution.py:251
  468.5 7.1 copy-start.39
  468.5 7.1 copy-start.43
  475.6 4.1 copy-start.19
  475.6 4.1 copy-start.38
  481.7 2.5 copy-start.9
  485.9 0.7 copy-start.29
  485.9 0.7 copy-start.30
  485.9 0.7 copy-start.31
  485.9 3.3 copy-start.23
  485.9 3.3 copy-start.24
  485.9 3.3 copy-start.25
  485.9 3.3 copy-start.26
  486.0 3.3 copy-start.27
  486.0 45.2 %copy-start.32 = (f32[768]{0:T(1024)S(1)}, f32[768]{0:T(1024)}, u32[]{:S(2)}) copy-start(f32[768]{0:T(1024)} %get-tuple-element.275) | copy-start | bytes 9220
  486.0 65.1 %copy-start.3 = (f32[512,768]{1,0:T(8,128)S(1)}, f32[512,768]{1,0:T(8,128)}, u32[]{:S(2)}) copy-start(f32[512,768]{1,0:T(8,128)} %copy-done.2) | copy-start | bytes 4718596
  750.1 5.9 copy-start.15
  750.1 6.7 copy-start.13
  756.1 2.2 copy-start.12
Sparse Core Ops, SparseCore 0:
  9.6 29.5 all-gather.4
  80.9 58.3 reduce-scatter.4
  143.7 28.4 all-gather.6
  196.0 37.9 reduce-scatter.6
  240.5 28.5 all-gather.8
  282.5 37.9 reduce-scatter.8
  327.1 28.5 all-gather.10
  468.3 38.6 reduce-scatter.10
  513.2 236.8 all-reduce.4
where the time goes:
time: 779 us; the launch traced here: 767 us
  waiting for transfers between devices  439 us (56%)
  matrix products  150 us (19%)
  blocking collectives  60.5 us (8%)
  local copies, waits for them, and re-layouts  55.8 us (7%)
  other arithmetic  45.1 us (6%)
  between operations  15.5 us (2%)
    psum x1, waiting for transfers between devices, body(): lax.psum((query_weight_grad, key_weight_grad, value_weight_grad, query_bi...  197 us
    reduce_scatter x1, waiting for transfers between devices, body(): lax.psum_scatter(jnp.dot(attended, mixer_weight, preferred_element_type=j...  57.9 us
    psum x1, blocking collectives, body(): lax.psum((mixer_bias_grad, first_gain_grad, first_shift_grad, outer_bias_...  40.6 us
    reduce_scatter x1, waiting for transfers between devices, body(): lax.psum_scatter(jnp.einsum('gf,df->gd', inner_low, inner_weight, preferr...  37.9 us
    reduce_scatter x1, waiting for transfers between devices, body(): lax.psum_scatter(jnp.dot(activated, outer_weight, preferred_element_type=...  34.2 us
    all_gather x1, waiting for transfers between devices, body(): lax.all_gather(second_grad.astype(jnp.bfloat16), 'tensor', axis=0, tiled=...  28.6 us
    all_gather x1, waiting for transfers between devices, body(): lax.all_gather(first_grad.astype(jnp.bfloat16), 'tensor', axis=0, tiled=T...  28.6 us
    all_gather x1, waiting for transfers between devices, body(): normed_all = lax.all_gather(normed_low, 'tensor', axis=0, tiled=True)  27.2 us
  transfers between devices with their start and end apart: 9, of which 8 were waited for; matrix products, arithmetic and copies ran while one was open for 4% of the time, Pallas kernels for 0%

commit v1 on v0

v1 whole, which is shorter than its diff:
```python
import jax
import jax.numpy as jnp
from jax import lax
from jax.experimental import pallas as pl
from jax.experimental.pallas import tpu as pltpu
from jax.sharding import PartitionSpec as P

D = 768
HEAD_DIM = 64
L = 512

eps_norm = 1e-06
root_half = 0.7071067811865476
inv_root_tau = 0.3989422804014327
low_type = jnp.bfloat16
wide = jnp.float32
NN = (((1,), (0,)), ((), ()))
NT = (((1,), (1,)), ((), ()))
TN = (((0,), (0,)), ((), ()))


def product(left, right, dims):
    return lax.dot_general(left, right, dims, preferred_element_type=wide)


def layer_norm(token_rows, norm_gain, norm_shift):
    center = token_rows - jnp.mean(token_rows, axis=-1, keepdims=True)
    inverse = lax.rsqrt(jnp.mean(center * center, axis=-1, keepdims=True) + eps_norm)
    normed = center * inverse
    return (normed * norm_gain + norm_shift, normed, inverse)


def norm_backward(incoming, normed, inverse, norm_gain):
    scaled = incoming * norm_gain
    middle = jnp.mean(scaled, axis=-1, keepdims=True)
    along = jnp.mean(scaled * normed, axis=-1, keepdims=True)
    return inverse * (scaled - middle - normed * along)


def attend_forward(tokens, projection, owner_column, owner_row):
    width = projection.shape[0] // 3 // HEAD_DIM * HEAD_DIM
    heads = width // HEAD_DIM

    def kernel(tokens_ref, projection_ref, column_ref, row_ref, qkv_ref, attended_ref, probs_ref, mask):
        bias = projection_ref[3 * width : 3 * width + 1, : 3 * width].astype(wide)
        qkv_ref[...] = (
            product(tokens_ref[...], projection_ref[: 3 * width, :], NT) + bias
        ).astype(low_type)
        row = lax.broadcasted_iota(jnp.int32, (L, L), 0)
        column = lax.broadcasted_iota(jnp.int32, (L, L), 1)
        allowed = (column_ref[...] == row_ref[...]) | (row == column)
        mask[...] = jnp.where(allowed, 0.0, -1e30)
        for head in range(heads):
            at = head * HEAD_DIM
            queries = qkv_ref[:, at : at + HEAD_DIM] * jnp.asarray(HEAD_DIM**-0.5, low_type)
            key_rows = qkv_ref[:, width + at : width + at + HEAD_DIM]
            values = qkv_ref[:, 2 * width + at : 2 * width + at + HEAD_DIM]
            scores = product(queries, key_rows, NT) + mask[...]
            highest = jnp.max(scores, axis=-1, keepdims=True)
            expanded = jnp.exp(scores - highest)
            row_total = jnp.sum(expanded, axis=-1, keepdims=True)
            probs = (expanded * (1.0 / row_total)).astype(low_type)
            probs_ref[head] = probs
            attended_ref[:, at : at + HEAD_DIM] = product(probs, values, NN).astype(low_type)

    return pl.pallas_call(
        kernel,
        out_shape=(
            jax.ShapeDtypeStruct((L, 3 * width), low_type),
            jax.ShapeDtypeStruct((L, width), low_type),
            jax.ShapeDtypeStruct((heads, L, L), low_type),
        ),
        scratch_shapes=[pltpu.VMEM((L, L), wide)],
        cost_estimate=pl.CostEstimate(
            flops=9 * L * D * width, transcendentals=heads * L * L, bytes_accessed=16000000
        ),
        name="attend_forward",
    )(tokens, projection, owner_column, owner_row)


def attend_backward(branch_low, mixer, qkv, attended, probs):
    width = attended.shape[1]
    heads = width // HEAD_DIM

    def kernel(branch_ref, mixer_ref, qkv_ref, attended_ref, probs_ref, grad_ref):
        attended_grad = product(branch_ref[...], mixer_ref[:width, :], NT).astype(low_type)
        for head in range(heads):
            at = head * HEAD_DIM
            queries = qkv_ref[:, at : at + HEAD_DIM] * jnp.asarray(HEAD_DIM**-0.5, low_type)
            key_rows = qkv_ref[:, width + at : width + at + HEAD_DIM]
            values = qkv_ref[:, 2 * width + at : 2 * width + at + HEAD_DIM]
            grad = attended_grad[:, at : at + HEAD_DIM]
            along = attended_ref[:, at : at + HEAD_DIM].astype(wide) * grad.astype(wide)
            row_dot = jnp.sum(along, axis=-1, keepdims=True)
            probs = probs_ref[head]
            probs_grad = product(grad, values, NT)
            scores_grad = (probs.astype(wide) * (probs_grad - row_dot)).astype(low_type)
            grad_ref[:, at : at + HEAD_DIM] = (
                product(scores_grad, key_rows, NN) * (HEAD_DIM**-0.5)
            ).astype(low_type)
            grad_ref[:, width + at : width + at + HEAD_DIM] = product(
                scores_grad, queries, TN
            ).astype(low_type)
            grad_ref[:, 2 * width + at : 2 * width + at + HEAD_DIM] = product(
                probs, grad, TN
            ).astype(low_type)

    return pl.pallas_call(
        kernel,
        out_shape=jax.ShapeDtypeStruct((L, 3 * width), low_type),
        cost_estimate=pl.CostEstimate(
            flops=9 * L * D * width, transcendentals=0, bytes_accessed=16000000
        ),
        name="attend_backward",
    )(branch_low, mixer, qkv, attended, probs)


def inner_forward(normed_low, weights, start):
    block = L // 2
    rows = weights.shape[0]

    def kernel(normed_ref, weights_ref, activated_ref, slope_ref):
        inner_pre = product(
            normed_ref[...], weights_ref[start : start + D, :], NN
        ) + weights_ref[start + D : start + D + 1, :].astype(wide)
        below = 0.5 * (1.0 + lax.erf(inner_pre * root_half))
        density = jnp.exp(-0.5 * inner_pre * inner_pre) * inv_root_tau
        activated_ref[...] = (inner_pre * below).astype(low_type)
        slope_ref[...] = (below + inner_pre * density).astype(low_type)

    return pl.pallas_call(
        kernel,
        grid=(L // block,),
        out_shape=(jax.ShapeDtypeStruct((L, D), low_type),) * 2,
        in_specs=[
            pl.BlockSpec((block, D), lambda i: (i, 0)),
            pl.BlockSpec((rows, D), lambda i: (0, 0)),
        ],
        out_specs=[pl.BlockSpec((block, D), lambda i: (i, 0))] * 2,
        cost_estimate=pl.CostEstimate(
            flops=8 * L * D * D, transcendentals=2 * L * D, bytes_accessed=16000000
        ),
        name="inner_forward",
    )(normed_low, weights)


def solution(mesh):
    dp_size = mesh.shape["dp"]
    tensor_size = mesh.shape["tensor"]
    masks = [1, 2, 6] + [1 << bit for bit in range(3, 16)]
    masks = masks[: dp_size.bit_length() - 1]

    def over_tensor(value, mask):
        return lax.ppermute(value, "tensor", [(i, i ^ mask) for i in range(tensor_size)])

    def over_dp(value, mask):
        return lax.ppermute(value, "dp", [(i, i ^ mask) for i in range(dp_size)])

    def gather_slots(own):
        first = over_tensor(own, 1)
        second = over_tensor(own, 2)
        return [own, first, second, over_tensor(second, 1)]

    def add_low(left, right):
        return (left.astype(wide) + right.astype(wide)).astype(low_type)

    def reduce_weight(kept, sent):
        total = add_low(kept, over_tensor(sent, 2))
        for mask in masks[:-1]:
            total = add_low(total, over_dp(total, mask))
        return total.astype(wide) + over_dp(total, masks[-1]).astype(wide)

    def body(
        tokens,
        grad_out,
        lengths,
        segment_ids,
        query_weight,
        query_bias,
        key_weight,
        value_weight,
        value_bias,
        mixer_weight,
        mixer_bias,
        first_gain,
        first_shift,
        inner_weight,
        inner_bias,
        outer_weight,
        outer_bias,
        second_gain,
        second_shift,
    ):
        width = query_weight.shape[1]
        place = lax.axis_index("tensor")
        bias_row = jnp.concatenate([query_bias, jnp.zeros_like(query_bias), value_bias])
        bias_row = jnp.pad(bias_row[None, :], ((0, 15), (0, D - 3 * width)))
        own_projection = jnp.concatenate(
            [query_weight.T, key_weight.T, value_weight.T, bias_row], axis=0
        )
        own_middle = jnp.concatenate(
            [mixer_weight, inner_weight, jnp.pad(inner_bias[None, :], ((0, 15), (0, 0)))], axis=0
        )
        projections = gather_slots(own_projection)
        middles = gather_slots(own_middle)
        outers = gather_slots(outer_weight)

        segment_row = lax.dynamic_index_in_dim(segment_ids, place, 0, keepdims=False)
        own_length = lax.dynamic_index_in_dim(lengths, place, 0, keepdims=False)
        position = jnp.arange(L, dtype=jnp.int32)
        live = position < own_length
        owner_column = segment_row[:, None]
        owner_row = jnp.where(live, segment_row, -1)[None, :]

        heads_out = [attend_forward(tokens, w, owner_column, owner_row) for w in projections]
        attn_branch = mixer_bias.astype(wide)
        for (_, attended, _), weights in zip(heads_out, middles):
            attn_branch = attn_branch + product(attended, weights[:width], NN)
        token_float = tokens.astype(wide)
        normed_one, first_hat, first_inverse = layer_norm(
            token_float + attn_branch, first_gain, first_shift
        )
        normed_low = normed_one.astype(low_type)
        hidden = [inner_forward(normed_low, weights, width) for weights in middles]
        ffn_branch = outer_bias.astype(wide)
        for (activated, _), weights in zip(hidden, outers):
            ffn_branch = ffn_branch + product(activated, weights, NN)
        layer_out, second_hat, second_inverse = layer_norm(
            normed_one + ffn_branch, second_gain, second_shift
        )
        valid = live.astype(wide)[:, None]
        stat_terms = jnp.stack(
            [
                jnp.sum(valid * token_float * token_float),
                jnp.sum(valid * attn_branch * attn_branch),
                jnp.sum(valid * ffn_branch * ffn_branch),
                jnp.sum(valid),
            ]
        )
        incoming = grad_out.astype(wide)
        second_gain_grad = jnp.sum(incoming * second_hat, axis=0)
        second_shift_grad = jnp.sum(incoming, axis=0)
        second_grad = norm_backward(incoming, second_hat, second_inverse, second_gain)
        outer_bias_grad = jnp.sum(second_grad, axis=0)
        ffn_low = second_grad.astype(low_type)

        def pair_product(left, right, left_other, right_other):
            return (
                product(left, right, TN) + product(left_other, right_other, TN)
            ).astype(low_type)

        ffn_other = over_tensor(ffn_low, 1)
        normed_other = over_tensor(normed_low, 1)
        activated_other = {j: over_tensor(hidden[j ^ 1][0], 1) for j in (0, 2)}
        outer_parts = {
            j: pair_product(hidden[j][0], ffn_low, activated_other[j], ffn_other) for j in (2, 0)
        }
        outer_weight_grad = reduce_weight(outer_parts[0], outer_parts[2])

        normed_grad = second_grad
        inner_lows, inner_bias_rows = [], []
        for (_, slope), outer, middle in zip(hidden, outers, middles):
            inner_grad = product(ffn_low, outer, NT) * slope.astype(wide)
            inner_bias_rows.append(jnp.sum(inner_grad, axis=0))
            inner_lows.append(inner_grad.astype(low_type))
        inner_other = {j: over_tensor(inner_lows[j ^ 1], 1) for j in (0, 2)}
        inner_parts = {
            j: pair_product(normed_low, inner_lows[j], normed_other, inner_other[j]) for j in (2, 0)
        }
        inner_weight_grad = reduce_weight(inner_parts[0], inner_parts[2])
        for inner_low, middle in zip(inner_lows, middles):
            normed_grad = normed_grad + product(inner_low, middle[width : width + D], NT)

        first_gain_grad = jnp.sum(normed_grad * first_hat, axis=0)
        first_shift_grad = jnp.sum(normed_grad, axis=0)
        first_grad = norm_backward(normed_grad, first_hat, first_inverse, first_gain)
        mixer_bias_grad = jnp.sum(first_grad, axis=0)
        branch_low = first_grad.astype(low_type)
        branch_other = over_tensor(branch_low, 1)
        attended_other = {j: over_tensor(heads_out[j ^ 1][1], 1) for j in (0, 2)}
        mixer_parts = {
            j: pair_product(heads_out[j][1], branch_low, attended_other[j], branch_other)
            for j in (2, 0)
        }
        mixer_weight_grad = reduce_weight(mixer_parts[0], mixer_parts[2])

        qkv_grads = [
            attend_backward(branch_low, middle, *kept)
            for kept, middle in zip(heads_out, middles)
        ]
        tokens_other = over_tensor(tokens, 1)
        qkv_other = {j: over_tensor(qkv_grads[j ^ 1], 1) for j in (0, 2)}
        qkv_parts = {
            j: pair_product(qkv_grads[j], tokens, qkv_other[j], tokens_other) for j in (2, 0)
        }
        qkv_weight_grad = reduce_weight(qkv_parts[0], qkv_parts[2])
        tokens_grad = first_grad
        for qkv_grad, projection in zip(qkv_grads, projections):
            tokens_grad = tokens_grad + product(qkv_grad, projection[: 3 * width], NN)

        def lane_pad(row):
            return jnp.pad(row, (0, D - row.shape[0]))

        bias_rows = [jnp.sum(qkv_grad.astype(wide), axis=0) for qkv_grad in qkv_grads]
        small = jnp.stack(
            [
                mixer_bias_grad,
                first_gain_grad,
                first_shift_grad,
                outer_bias_grad,
                second_gain_grad,
                second_shift_grad,
                lane_pad(stat_terms),
                jnp.zeros((D,), wide),
            ]
            + inner_bias_rows
            + [lane_pad(row) for row in bias_rows]
        )

        def reorder(rows, mask):
            slots = [8 + (j ^ mask) for j in range(4)] + [12 + (j ^ mask) for j in range(4)]
            return jnp.concatenate([rows[:8]] + [rows[i : i + 1] for i in slots])

        small = small + reorder(over_tensor(small, 1), 1)
        small = small + reorder(over_tensor(small, 2), 2)
        for mask in masks:
            small = small + over_dp(small, mask)
        statistics = jnp.sqrt(small[6, :3] / (small[6, 3] * D))
        return (
            layer_out.astype(low_type),
            tokens_grad,
            qkv_weight_grad[:width].T,
            small[12, :width],
            qkv_weight_grad[width : 2 * width].T,
            qkv_weight_grad[2 * width :].T,
            small[12, 2 * width : 3 * width],
            mixer_weight_grad,
            small[0],
            small[1],
            small[2],
            inner_weight_grad,
            small[8],
            outer_weight_grad,
            small[3],
            small[4],
            small[5],
            statistics,
        )

    in_specs = (
        P(("dp", "tensor"), None),
        P(("dp", "tensor"), None),
        P("dp"),
        P("dp", None),
        P(None, "tensor"),
        P("tensor"),
        P(None, "tensor"),
        P(None, "tensor"),
        P("tensor"),
        P("tensor", None),
        P(),
        P(),
        P(),
        P(None, "tensor"),
        P("tensor"),
        P("tensor", None),
        P(),
        P(),
        P(),
    )
    out_specs = (
        P(("dp", "tensor"), None),
        P(("dp", "tensor"), None),
        P(None, "tensor"),
        P("tensor"),
        P(None, "tensor"),
        P(None, "tensor"),
        P("tensor"),
        P("tensor", None),
        P(),
        P(),
        P(),
        P(None, "tensor"),
        P("tensor"),
        P("tensor", None),
        P(),
        P(),
        P(),
        P(),
    )
    return jax.shard_map(body, mesh=mesh, in_specs=in_specs, out_specs=out_specs, check_vma=False)
```

time: 779 us -> 515 us (0.66)
  waiting for transfers between devices: 439 us -> 296 us
  matrix products: 150 us -> 73.3 us
  Pallas kernels: 0 us -> 62.4 us
  blocking collectives: 60.5 us -> 0 us
  local copies, waits for them, and re-layouts: 55.8 us -> 15.4 us
  starting transfers between devices: 1.01 us -> 28.4 us
  other arithmetic: 45.1 us -> 26.4 us
  between operations: 15.5 us -> 2.87 us
    ppermute x0 -> x42, waiting for transfers between devices: none -> 296 us  [the longest x15 187 us: over_dp(): return lax.ppermute(value, 'dp', [(i, i ^ mask) for i in range(dp_size)])]
    psum x1 -> x0, waiting for transfers between devices: 197 us -> none  [body(): lax.psum((query_weight_grad, key_weight_grad, value_weight_grad, query_bi...]
    reduce_scatter x4 -> x0, waiting for transfers between devices: 130 us -> none  [the longest x1 57.9 us: body(): lax.psum_scatter(jnp.dot(attended, mixer_weight, preferred_element_type=j...]
    all_gather x4 -> x0, waiting for transfers between devices: 111 us -> none  [the longest x1 28.6 us: body(): lax.all_gather(second_grad.astype(jnp.bfloat16), 'tensor', axis=0, tiled=...]
    dot_general x40 -> x36, matrix products: 150 us -> 73.3 us  [product(): return lax.dot_general(left, right, dims, preferred_element_type=wide)]
    pallas_call x0 -> x12, Pallas kernels: none -> 62.4 us  [the longest x4 26.7 us: attend_backward(): pl.pallas_call(kernel, out_shape=jax.ShapeDtypeStruct((L, 3 * width), low...]
    psum x2 -> x0, blocking collectives: 60.5 us -> none  [the longest x1 40.6 us: body(): lax.psum((mixer_bias_grad, first_gain_grad, first_shift_grad, outer_bias_...]
    ppermute x0 -> x42, starting transfers between devices: none -> 28.4 us  [the longest x15 16.4 us: over_dp(): return lax.ppermute(value, 'dp', [(i, i ^ mask) for i in range(dp_size)])]
  transfers between devices with their start and end apart: 9 -> 42, of which waited for: 8 -> 14; matrix products, arithmetic and copies ran while one was open for 4% -> 21% of each run, Pallas kernels for 0% -> 12%
where the time goes in v1:
time: 515 us; the launch traced here: 505 us
  waiting for transfers between devices  296 us (57%)
  matrix products  73.3 us (14%)
  Pallas kernels  62.4 us (12%)
  starting transfers between devices  28.4 us (6%)
  other arithmetic  26.4 us (5%)
  local copies, waits for them, and re-layouts  15.4 us (3%)
    ppermute x15, waiting for transfers between devices, over_dp(): return lax.ppermute(value, 'dp', [(i, i ^ mask) for i in range(dp_size)])  187 us
    ppermute x27, waiting for transfers between devices, over_tensor(): lax.ppermute(value, 'tensor', [(i, i ^ mask) for i in range(tensor_size)])  109 us
    dot_general x36, matrix products, product(): return lax.dot_general(left, right, dims, preferred_element_type=wide)  73.3 us
    pallas_call x4, Pallas kernels, attend_backward(): pl.pallas_call(kernel, out_shape=jax.ShapeDtypeStruct((L, 3 * width), low...  26.7 us
    pallas_call x4, Pallas kernels, attend_forward(): pl.pallas_call(kernel, out_shape=(jax.ShapeDtypeStruct((L, 3 * width), lo...  20.7 us
    ppermute x15, starting transfers between devices, over_dp(): return lax.ppermute(value, 'dp', [(i, i ^ mask) for i in range(dp_size)])  16.4 us
    pallas_call x4, Pallas kernels, inner_forward(): pl.pallas_call(kernel, grid=(L // block,), out_shape=(jax.ShapeDtypeStruc...  15 us
    ppermute x27, starting transfers between devices, over_tensor(): lax.ppermute(value, 'tensor', [(i, i ^ mask) for i in range(tensor_size)])  12.1 us
  transfers between devices with their start and end apart: 42, of which 14 were waited for; matrix products, arithmetic and copies ran while one was open for 21% of the time, Pallas kernels for 12%

profile of v1, /device:TPU:16, one launch (start us, length us, event | category | flops | bytes accessed | tf_op | source)
XLA Modules:
  0.0 504.5 jit_solution(5518577337552285031)
XLA Ops:
  3.0 1.6 collective-permute-start.3
  6.7 32.2 %collective-permute-done.3.weights_ref.mixer_ref = bf16[976,768]{1,0:T(8,128)(2,1)} collective-permute-done((bf16[976,768]{1,0:T(8,128)(2,1)S(1)}, bf16[976,768]{1,0:T(8,128)(2,1)}, u32[]{:S(2)}, u32[]{:S(2)}) %collective-permute-start.3) | collective-permute-done | bytes 1499168 | tf_op jit(solution)/shard_map/ppermute | solution.py:154
  40.9 1.9 compare_select_fusion
  45.1 5.2 %attend_forward.4 = (bf16[512,576]{1,0:T(8,128)(2,1)}, bf16[512,192]{1,0:T(8,128)(2,1)}, bf16[3,512,512]{2,1,0:T(8,128)(2,1)}) custom-call(bf16[512,768]{1,0:T(8,128)(2,1)} %tokens_ref.7, bf16[592,768]{1,0:T(8,128)(2,1)} %fusion.25.projection_ref, s32[512,1]{1,0:T(8,128)} %copy.41.column_ref, s32[1,512]{1,0:T(1,128)} %get-tuple-element.108.row_ref), custom_call_target="tpu_custom_call" | custom-call | flops 679477248 | bytes 16000000 | tf_op jit(solution)/shard_map/attend_forward/pallas_call | solution.py:66
  50.9 7.4 %collective-permute-done.2.projection_ref = bf16[592,768]{1,0:T(8,128)(2,1)} collective-permute-done((bf16[592,768]{1,0:T(8,128)(2,1)}, bf16[592,768]{1,0:T(8,128)(2,1)}, u32[]{:S(2)}, u32[]{:S(2)}) %collective-permute-start.2) | collective-permute-done | bytes 909344 | tf_op jit(solution)/shard_map/ppermute | solution.py:154
  58.4 2.5 fusion.67
  60.8 5.2 %attend_forward.6 = (bf16[512,576]{1,0:T(8,128)(2,1)}, bf16[512,192]{1,0:T(8,128)(2,1)}, bf16[3,512,512]{2,1,0:T(8,128)(2,1)}) custom-call(bf16[512,768]{1,0:T(8,128)(2,1)} %tokens_ref.7, bf16[592,768]{1,0:T(8,128)(2,1)} %collective-permute-done.2.projection_ref, s32[512,1]{1,0:T(8,128)} %copy.41.column_ref, s32[1,512]{1,0:T(1,128)} %get-tuple-element.108.row_ref), custom_call_target="tpu_custom_call" | custom-call | flops 679477248 | bytes 16000000 | tf_op jit(solution)/shard_map/attend_forward/pallas_call | solution.py:66
  66.5 5.2 %attend_forward.5 = (bf16[512,576]{1,0:T(8,128)(2,1)}, bf16[512,192]{1,0:T(8,128)(2,1)}, bf16[3,512,512]{2,1,0:T(8,128)(2,1)}) custom-call(bf16[512,768]{1,0:T(8,128)(2,1)} %tokens_ref.7, bf16[592,768]{1,0:T(8,128)(2,1)} %collective-permute-done.projection_ref, s32[512,1]{1,0:T(8,128)} %copy.41.column_ref, s32[1,512]{1,0:T(1,128)} %get-tuple-element.108.row_ref), custom_call_target="tpu_custom_call" | custom-call | flops 679477248 | bytes 16000000 | tf_op jit(solution)/shard_map/attend_forward/pallas_call | solution.py:66
  71.7 2.5 fusion.45
  74.2 2.6 fusion.47
  76.8 5.7 %collective-permute-done.7 = bf16[768,768]{1,0:T(8,128)(2,1)} collective-permute-done((bf16[768,768]{1,0:T(8,128)(2,1)}, bf16[768,768]{1,0:T(8,128)(2,1)}, u32[]{:S(2)}, u32[]{:S(2)}) %collective-permute-start.7) | collective-permute-done | bytes 1179680 | tf_op jit(solution)/shard_map/ppermute | solution.py:154
  83.0 5.2 %attend_forward.7 = (bf16[512,576]{1,0:T(8,128)(2,1)}, bf16[512,192]{1,0:T(8,128)(2,1)}, bf16[3,512,512]{2,1,0:T(8,128)(2,1)}) custom-call(bf16[512,768]{1,0:T(8,128)(2,1)} %tokens_ref.7, bf16[592,768]{1,0:T(8,128)(2,1)} %collective-permute-done.4.projection_ref, s32[512,1]{1,0:T(8,128)} %copy.41.column_ref, s32[1,512]{1,0:T(1,128)} %get-tuple-element.108.row_ref), custom_call_target="tpu_custom_call" | custom-call | flops 679477248 | bytes 16000000 | tf_op jit(solution)/shard_map/attend_forward/pallas_call | solution.py:66
  89.3 3.4 fusion.59
  94.6 3.8 inner_forward.4
  98.3 3.7 inner_forward.7
  102.0 3.7 inner_forward.6
  105.8 3.8 inner_forward.5
  109.6 2.4 fusion.68
  111.9 2.1 fusion.70
  114.1 2.1 fusion.69
  116.2 3.9 fusion.9
  122.1 1.6 fusion.54
  125.1 2.2 fusion.65
  128.7 2.2 fusion.60
  130.9 2.4 fusion.66
  133.3 2.4 fusion.21
  135.8 2.1 fusion.61
  137.9 2.4 fusion.23
  140.3 1.6 multiply_reduce_fusion
  143.4 6.7 %attend_backward.4 = bf16[512,576]{1,0:T(8,128)(2,1)} custom-call(bf16[512,768]{1,0:T(8,128)(2,1)} %convert_element_type.268.branch_ref, bf16[976,768]{1,0:T(8,128)(2,1)} %copy-done.10, bf16[512,576]{1,0:T(8,128)(2,1)} %get-tuple-element.50.qkv_ref, bf16[512,192]{1,0:T(8,128)(2,1)} %get-tuple-element.38.attended_ref, ...), custom_call_target="tpu_custom_call" | custom-call | flops 679477248 | bytes 16000000 | tf_op jit(solution)/shard_map/attend_backward/pallas_call | solution.py:108
  150.1 3.1 fusion.31
  153.4 2.7 select_maximum_fusion
  156.1 6.8 %attend_backward.5 = bf16[512,576]{1,0:T(8,128)(2,1)} custom-call(bf16[512,768]{1,0:T(8,128)(2,1)} %convert_element_type.268.branch_ref, bf16[976,768]{1,0:T(8,128)(2,1)} %collective-permute-done.1.weights_ref.mixer_ref, bf16[512,576]{1,0:T(8,128)(2,1)} %get-tuple-element.52.qkv_ref, bf16[512,192]{1,0:T(8,128)(2,1)} %get-tuple-element.39.attended_ref, ...), custom_call_target="tpu_custom_call" | custom-call | flops 679477248 | bytes 16000000 | tf_op jit(solution)/shard_map/attend_backward/pallas_call | solution.py:108
  164.1 6.6 %attend_backward.6 = bf16[512,576]{1,0:T(8,128)(2,1)} custom-call(bf16[512,768]{1,0:T(8,128)(2,1)} %convert_element_type.268.branch_ref, bf16[976,768]{1,0:T(8,128)(2,1)} %collective-permute-done.3.weights_ref.mixer_ref, bf16[512,576]{1,0:T(8,128)(2,1)} %get-tuple-element.54.qkv_ref, bf16[512,192]{1,0:T(8,128)(2,1)} %get-tuple-element.40.attended_ref, ...), custom_call_target="tpu_custom_call" | custom-call | flops 679477248 | bytes 16000000 | tf_op jit(solution)/shard_map/attend_backward/pallas_call | solution.py:108
  172.0 6.7 %attend_backward.7 = bf16[512,576]{1,0:T(8,128)(2,1)} custom-call(bf16[512,768]{1,0:T(8,128)(2,1)} %convert_element_type.268.branch_ref, bf16[976,768]{1,0:T(8,128)(2,1)} %copy-done.11, bf16[512,576]{1,0:T(8,128)(2,1)} %get-tuple-element.56.qkv_ref, bf16[512,192]{1,0:T(8,128)(2,1)} %get-tuple-element.41.attended_ref, ...), custom_call_target="tpu_custom_call" | custom-call | flops 679477248 | bytes 16000000 | tf_op jit(solution)/shard_map/attend_backward/pallas_call | solution.py:108
  180.1 2.0 fusion.27
  182.2 2.1 fusion.29
  184.3 3.4 add_add_fusion
  188.6 1.6 collective-permute-start.17
  190.2 3.8 fusion.40
  195.3 1.6 collective-permute-start.18
  198.1 2.1 copy.46
  200.2 1.7 collective-permute-start.19
  201.9 3.6 fusion.75
  205.4 2.1 copy.45
  207.9 2.1 fusion.71
  210.0 3.0 collective-permute-done.20
  216.1 1.8 add_convert_fusion.14
  218.4 1.8 fusion.72
  220.2 1.9 add_convert_fusion.13
  222.7 1.9 add_convert_fusion.8
  229.2 2.0 add_convert_fusion.9
  231.2 16.0 %collective-permute-done.12 = bf16[576,768]{1,0:T(8,128)(2,1)S(1)} collective-permute-done((bf16[576,768]{1,0:T(8,128)(2,1)S(1)}, bf16[576,768]{1,0:T(8,128)(2,1)S(1)}, u32[]{:S(2)}, u32[]{:S(2)}) %collective-permute-start.12) | collective-permute-done | bytes 884768 | tf_op jit(solution)/shard_map/ppermute | solution.py:154
  247.5 25.0 %collective-permute-done.31 = bf16[768,768]{1,0:T(8,128)(2,1)S(1)} collective-permute-done((bf16[768,768]{1,0:T(8,128)(2,1)S(1)}, bf16[768,768]{1,0:T(8,128)(2,1)S(1)}, u32[]{:S(2)}, u32[]{:S(2)}) %collective-permute-start.31) | collective-permute-done | bytes 1179680 | tf_op jit(solution)/shard_map/ppermute | solution.py:154
  275.8 21.2 %collective-permute-done.38 = bf16[768,768]{1,0:T(8,128)(2,1)S(1)} collective-permute-done((bf16[768,768]{1,0:T(8,128)(2,1)S(1)}, bf16[768,768]{1,0:T(8,128)(2,1)S(1)}, u32[]{:S(2)}, u32[]{:S(2)}) %collective-permute-start.38) | collective-permute-done | bytes 1179680 | tf_op jit(solution)/shard_map/ppermute | solution.py:154
  302.0 18.4 %collective-permute-done.32 = bf16[768,768]{1,0:T(8,128)(2,1)S(1)} collective-permute-done((bf16[768,768]{1,0:T(8,128)(2,1)S(1)}, bf16[768,768]{1,0:T(8,128)(2,1)S(1)}, u32[]{:S(2)}, u32[]{:S(2)}) %collective-permute-start.32) | collective-permute-done | bytes 1179680 | tf_op jit(solution)/shard_map/ppermute | solution.py:157
  324.0 21.6 %collective-permute-done.39 = bf16[768,768]{1,0:T(8,128)(2,1)S(1)} collective-permute-done((bf16[768,768]{1,0:T(8,128)(2,1)S(1)}, bf16[768,768]{1,0:T(8,128)(2,1)S(1)}, u32[]{:S(2)}, u32[]{:S(2)}) %collective-permute-start.39) | collective-permute-done | bytes 1179680 | tf_op jit(solution)/shard_map/ppermute | solution.py:157
  351.7 1.7 collective-permute-start.34
  353.4 27.8 %collective-permute-done.26 = bf16[192,768]{1,0:T(8,128)(2,1)S(1)} collective-permute-done((bf16[192,768]{1,0:T(8,128)(2,1)S(1)}, bf16[192,768]{1,0:T(8,128)(2,1)S(1)}, u32[]{:S(2)}, u32[]{:S(2)}) %collective-permute-start.26) | collective-permute-done | bytes 294944 | tf_op jit(solution)/shard_map/ppermute | solution.py:157
  381.7 2.1 collective-permute-start.41
  383.8 97.3 %collective-permute-done.27 = bf16[192,768]{1,0:T(8,128)(2,1)S(1)} collective-permute-done((bf16[192,768]{1,0:T(8,128)(2,1)S(1)}, bf16[192,768]{1,0:T(8,128)(2,1)S(1)}, u32[]{:S(2)}, u32[]{:S(2)}) %collective-permute-start.27) | collective-permute-done | bytes 294944 | tf_op jit(solution)/shard_map/ppermute | solution.py:157
  483.4 1.7 convert_add_fusion.1
  485.0 17.5 %collective-permute-done.41 = bf16[768,768]{1,0:T(8,128)(2,1)S(1)} collective-permute-done((bf16[768,768]{1,0:T(8,128)(2,1)S(1)}, bf16[768,768]{1,0:T(8,128)(2,1)S(1)}, u32[]{:S(2)}, u32[]{:S(2)}) %collective-permute-start.41) | collective-permute-done | bytes 1179680 | tf_op jit(solution)/shard_map/ppermute | solution.py:157
  502.5 1.7 convert_add_fusion
  (271 shorter events, 56.4 us)
Async XLA Ops:
  2.9 47.4 %copy-start.10 = (bf16[976,768]{1,0:T(8,128)(2,1)}, bf16[976,768]{1,0:T(8,128)(2,1)S(1)}, u32[]{:S(2)}) copy-start(bf16[976,768]{1,0:T(8,128)(2,1)S(1)} %fusion.12.weights_ref.mixer_ref) | copy-start | bytes 4497412
  2.9 37.5 %copy-start.51 = (s32[4]{0:T(128)S(1)}, s32[4]{0:T(128)}, u32[]{:S(2)}) copy-start(s32[4]{0:T(128)} %param.21) | copy-start | bytes 52
  2.9 42.1 %copy-start.39 = (bf16[768]{0:T(1024)(128)(2,1)S(1)}, bf16[768]{0:T(1024)(128)(2,1)}, u32[]{:S(2)}) copy-start(bf16[768]{0:T(1024)(128)(2,1)} %param.29) | copy-start | bytes 4612
  2.9 42.1 %copy-start.40 = (bf16[768]{0:T(1024)(128)(2,1)S(1)}, bf16[768]{0:T(1024)(128)(2,1)}, u32[]{:S(2)}) copy-start(bf16[768]{0:T(1024)(128)(2,1)} %param.31) | copy-start | bytes 4612
  2.9 42.0 %copy-start.41 = (bf16[768]{0:T(1024)(128)(2,1)S(1)}, bf16[768]{0:T(1024)(128)(2,1)}, u32[]{:S(2)}) copy-start(bf16[768]{0:T(1024)(128)(2,1)} %param.30) | copy-start | bytes 4612
  3.0 42.1 %copy-start.42 = (bf16[768]{0:T(1024)(128)(2,1)S(1)}, bf16[768]{0:T(1024)(128)(2,1)}, u32[]{:S(2)}) copy-start(bf16[768]{0:T(1024)(128)(2,1)} %param.35) | copy-start | bytes 4612
  3.0 42.1 %copy-start.43 = (bf16[768]{0:T(1024)(128)(2,1)S(1)}, bf16[768]{0:T(1024)(128)(2,1)}, u32[]{:S(2)}) copy-start(bf16[768]{0:T(1024)(128)(2,1)} %param.36) | copy-start | bytes 4612
  3.0 42.1 %copy-start.44 = (bf16[768]{0:T(1024)(128)(2,1)S(1)}, bf16[768]{0:T(1024)(128)(2,1)}, u32[]{:S(2)}) copy-start(bf16[768]{0:T(1024)(128)(2,1)} %param.37) | copy-start | bytes 4612
  3.0 35.9 %collective-permute-start.3 = (bf16[976,768]{1,0:T(8,128)(2,1)S(1)}, bf16[976,768]{1,0:T(8,128)(2,1)}, u32[]{:S(2)}, u32[]{:S(2)}) collective-permute-start(bf16[976,768]{1,0:T(8,128)(2,1)S(1)} %fusion.12.weights_ref.mixer_ref), channel_id=1, source_target_pairs={{0,2},{1,3},{2,0},{3,1},{4,6},{5,7},{6,4},{7,5},{8,10},{9,11},{10,... | collective-permute-start | bytes 4497416 | tf_op jit(solution)/shard_map/ppermute | solution.py:154
  5.6 52.7 %copy-start.21 = (bf16[192,768]{1,0:T(8,128)(2,1)S(1)}, bf16[192,768]{1,0:T(8,128)(2,1)}, u32[]{:S(2)}) copy-start(bf16[192,768]{1,0:T(8,128)(2,1)} %param.28) | copy-start | bytes 884740
  5.6 52.7 %collective-permute-start.2 = (bf16[592,768]{1,0:T(8,128)(2,1)}, bf16[592,768]{1,0:T(8,128)(2,1)}, u32[]{:S(2)}, u32[]{:S(2)}) collective-permute-start(bf16[592,768]{1,0:T(8,128)(2,1)} %fusion.25.projection_ref), channel_id=1, source_target_pairs={{0,2},{1,3},{2,0},{3,1},{4,6},{5,7},{6,4},{7,5},{8,10},{9,11},{10,... | collective-permute-start | bytes 2727944 | tf_op jit(solution)/shard_map/ppermute | solution.py:154
  6.2 68.0 %collective-permute-start.1 = (bf16[976,768]{1,0:T(8,128)(2,1)S(1)}, bf16[976,768]{1,0:T(8,128)(2,1)}, u32[]{:S(2)}, u32[]{:S(2)}) collective-permute-start(bf16[976,768]{1,0:T(8,128)(2,1)S(1)} %fusion.12.weights_ref.mixer_ref), channel_id=1, source_target_pairs={{0,1},{1,0},{2,3},{3,2},{4,5},{5,4},{6,7},{7,6},{8,9},{9,8},{10,11... | collective-permute-start | bytes 4497416 | tf_op jit(solution)/shard_map/ppermute | solution.py:154
  6.2 59.8 %collective-permute-start = (bf16[592,768]{1,0:T(8,128)(2,1)}, bf16[592,768]{1,0:T(8,128)(2,1)}, u32[]{:S(2)}, u32[]{:S(2)}) collective-permute-start(bf16[592,768]{1,0:T(8,128)(2,1)} %fusion.25.projection_ref), channel_id=1, source_target_pairs={{0,1},{1,0},{2,3},{3,2},{4,5},{5,4},{6,7},{7,6},{8,9},{9,8},{10,11... | collective-permute-start | bytes 2727944 | tf_op jit(solution)/shard_map/ppermute | solution.py:154
  38.9 49.3 %collective-permute-start.5 = (bf16[976,768]{1,0:T(8,128)(2,1)}, bf16[976,768]{1,0:T(8,128)(2,1)S(1)}, u32[]{:S(2)}, u32[]{:S(2)}) collective-permute-start(bf16[976,768]{1,0:T(8,128)(2,1)} %collective-permute-done.3.weights_ref.mixer_ref), channel_id=1, source_target_pairs={{0,1},{1,0},{2,3},{3,2},{4,5},{5,4},{6,7},{7,6},{8,9},{9,8},{10,11... | collective-permute-start | bytes 4497416 | tf_op jit(solution)/shard_map/ppermute | solution.py:154
  38.9 43.6 %collective-permute-start.7 = (bf16[768,768]{1,0:T(8,128)(2,1)}, bf16[768,768]{1,0:T(8,128)(2,1)}, u32[]{:S(2)}, u32[]{:S(2)}) collective-permute-start(bf16[768,768]{1,0:T(8,128)(2,1)} %param.34), channel_id=1, source_target_pairs={{0,2},{1,3},{2,0},{3,1},{4,6},{5,7},{6,4},{7,5},{8,10},{9,11},{10,... | collective-permute-start | bytes 3538952 | tf_op jit(solution)/shard_map/ppermute | solution.py:154
  58.3 24.1 %collective-permute-start.4 = (bf16[592,768]{1,0:T(8,128)(2,1)}, bf16[592,768]{1,0:T(8,128)(2,1)}, u32[]{:S(2)}, u32[]{:S(2)}) collective-permute-start(bf16[592,768]{1,0:T(8,128)(2,1)} %collective-permute-done.2.projection_ref), channel_id=1, source_target_pairs={{0,1},{1,0},{2,3},{3,2},{4,5},{5,4},{6,7},{7,6},{8,9},{9,8},{10,11... | collective-permute-start | bytes 2727944 | tf_op jit(solution)/shard_map/ppermute | solution.py:154
  66.0 48.1 %collective-permute-start.6 = (bf16[768,768]{1,0:T(8,128)(2,1)}, bf16[768,768]{1,0:T(8,128)(2,1)}, u32[]{:S(2)}, u32[]{:S(2)}) collective-permute-start(bf16[768,768]{1,0:T(8,128)(2,1)} %param.34), channel_id=1, source_target_pairs={{0,1},{1,0},{2,3},{3,2},{4,5},{5,4},{6,7},{7,6},{8,9},{9,8},{10,11... | collective-permute-start | bytes 3538952 | tf_op jit(solution)/shard_map/ppermute | solution.py:154
  74.2 141.2 %collective-permute-start.10 = (bf16[512,768]{1,0:T(8,128)(2,1)}, bf16[512,768]{1,0:T(8,128)(2,1)}, u32[]{:S(2)}, u32[]{:S(2)}) collective-permute-start(bf16[512,768]{1,0:T(8,128)(2,1)} %tokens_ref.7), channel_id=1, source_target_pairs={{0,1},{1,0},{2,3},{3,2},{4,5},{5,4},{6,7},{7,6},{8,9},{9,8},{10,11... | collective-permute-start | bytes 2359304 | tf_op jit(solution)/shard_map/ppermute | solution.py:154
  82.5 239.5 %collective-permute-start.21 = (bf16[512,192]{1,0:T(8,128)(2,1)}, bf16[512,192]{1,0:T(8,128)(2,1)}, u32[]{:S(2)}, u32[]{:S(2)}) collective-permute-start(bf16[512,192]{1,0:T(8,128)(2,1)} %get-tuple-element.39.attended_ref), channel_id=1, source_target_pairs={{0,1},{1,0},{2,3},{3,2},{4,5},{5,4},{6,7},{7,6},{8,9},{9,8},{10,11... | collective-permute-start | bytes 589832 | tf_op jit(solution)/shard_map/ppermute | solution.py:154
  82.5 33.7 %collective-permute-start.8 = (bf16[768,768]{1,0:T(8,128)(2,1)}, bf16[768,768]{1,0:T(8,128)(2,1)}, u32[]{:S(2)}, u32[]{:S(2)}) collective-permute-start(bf16[768,768]{1,0:T(8,128)(2,1)} %collective-permute-done.7), channel_id=1, source_target_pairs={{0,1},{1,0},{2,3},{3,2},{4,5},{5,4},{6,7},{7,6},{8,9},{9,8},{10,11... | collective-permute-start | bytes 3538952 | tf_op jit(solution)/shard_map/ppermute | solution.py:154
  123.8 12.0 %copy-start.8 = (bf16[512,768]{1,0:T(8,128)(2,1)}, bf16[512,768]{1,0:T(8,128)(2,1)S(1)}, u32[]{:S(2)}) copy-start(bf16[512,768]{1,0:T(8,128)(2,1)S(1)} %convert_element_type.259) | copy-start | bytes 2359300
  130.9 9.4 %copy-start.30 = (bf16[512,768]{1,0:T(8,128)(2,1)}, bf16[512,768]{1,0:T(8,128)(2,1)S(1)}, u32[]{:S(2)}) copy-start(bf16[512,768]{1,0:T(8,128)(2,1)S(1)} %get-tuple-element.89) | copy-start | bytes 2359300
  143.4 6.7 %copy-start.34 = (bf16[768,192]{0,1:T(8,128)(2,1)S(1)}, bf16[768,192]{0,1:T(8,128)(2,1)}, u32[]{:S(2)}) copy-start(bf16[768,192]{0,1:T(8,128)(2,1)} %param.26) | copy-start | bytes 884740
  143.4 6.7 %copy-start.36 = (bf16[768,192]{0,1:T(8,128)(2,1)S(1)}, bf16[768,192]{0,1:T(8,128)(2,1)}, u32[]{:S(2)}) copy-start(bf16[768,192]{0,1:T(8,128)(2,1)} %param.25) | copy-start | bytes 884740
  143.4 6.7 %copy-start.38 = (bf16[768,192]{0,1:T(8,128)(2,1)S(1)}, bf16[768,192]{0,1:T(8,128)(2,1)}, u32[]{:S(2)}) copy-start(bf16[768,192]{0,1:T(8,128)(2,1)} %param.23) | copy-start | bytes 884740
  172.0 8.2 %copy-start.5 = (bf16[512,576]{1,0:T(8,128)(2,1)S(1)}, bf16[512,576]{1,0:T(8,128)(2,1)}, u32[]{:S(2)}) copy-start(bf16[512,576]{1,0:T(8,128)(2,1)} %attend_backward.6) | copy-start | bytes 1769476
  180.0 8.5 %collective-permute-start.16 = (f32[16,768]{1,0:T(8,128)S(1)}, f32[16,768]{1,0:T(8,128)S(1)}, u32[]{:S(2)}, u32[]{:S(2)}) collective-permute-start(f32[16,768]{1,0:T(8,128)S(1)} %stack.83), channel_id=1, source_target_pairs={{0,1},{1,0},{2,3},{3,2},{4,5},{5,4},{6,7},{7,6},{8,9},{9,8},{10,11... | collective-permute-start | bytes 147464 | tf_op jit(solution)/shard_map/ppermute | solution.py:154
  188.6 8.3 %copy-start = (bf16[512,768]{1,0:T(8,128)(2,1)S(1)}, bf16[512,768]{1,0:T(8,128)(2,1)}, u32[]{:S(2)}) copy-start(bf16[512,768]{1,0:T(8,128)(2,1)} %convert_element_type.268.branch_ref) | copy-start | bytes 2359300
  188.6 8.3 %copy-start.16 = (bf16[512,192]{1,0:T(8,128)(2,1)S(1)}, bf16[512,192]{1,0:T(8,128)(2,1)}, u32[]{:S(2)}) copy-start(bf16[512,192]{1,0:T(8,128)(2,1)} %get-tuple-element.38.attended_ref) | copy-start | bytes 589828
  188.6 5.3 %collective-permute-start.17 = (f32[16,768]{1,0:T(8,128)S(1)}, f32[16,768]{1,0:T(8,128)S(1)}, u32[]{:S(2)}, u32[]{:S(2)}) collective-permute-start(f32[16,768]{1,0:T(8,128)S(1)} %add.236), channel_id=1, source_target_pairs={{0,2},{1,3},{2,0},{3,1},{4,6},{5,7},{6,4},{7,5},{8,10},{9,11},{10,... | collective-permute-start | bytes 147464 | tf_op jit(solution)/shard_map/ppermute | solution.py:154
  195.3 4.9 collective-permute-start.18
  200.2 21.9 %collective-permute-start.28 = (bf16[512,768]{1,0:T(8,128)(2,1)}, bf16[512,768]{1,0:T(8,128)(2,1)}, u32[]{:S(2)}, u32[]{:S(2)}) collective-permute-start(bf16[512,768]{1,0:T(8,128)(2,1)} %fusion.14.normed_ref), channel_id=1, source_target_pairs={{0,1},{1,0},{2,3},{3,2},{4,5},{5,4},{6,7},{7,6},{8,9},{9,8},{10,11... | collective-permute-start | bytes 2359304 | tf_op jit(solution)/shard_map/ppermute | solution.py:154
  200.2 7.6 %collective-permute-start.19 = (f32[16,768]{1,0:T(8,128)S(1)}, f32[16,768]{1,0:T(8,128)S(1)}, u32[]{:S(2)}, u32[]{:S(2)}) collective-permute-start(f32[16,768]{1,0:T(8,128)S(1)} %add.238), channel_id=1, source_target_pairs={{0,8},{4,12},{8,0},{12,4},{16,24},{20,28},{24,16},{28,20},{1,9},{5... | collective-permute-start | bytes 147464 | tf_op jit(solution)/shard_map/ppermute | solution.py:157
  207.6 8.4 %collective-permute-start.9 = (bf16[512,576]{0,1:T(8,128)(2,1)}, bf16[512,576]{0,1:T(8,128)(2,1)S(1)}, u32[]{:S(2)}, u32[]{:S(2)}) collective-permute-start(bf16[512,576]{0,1:T(8,128)(2,1)} %copy.45), channel_id=1, source_target_pairs={{0,1},{1,0},{2,3},{3,2},{4,5},{5,4},{6,7},{7,6},{8,9},{9,8},{10,11... | collective-permute-start | bytes 1769480 | tf_op jit(solution)/shard_map/ppermute | solution.py:154
  207.8 7.6 %copy-start.31 = (bf16[512,768]{1,0:T(8,128)(2,1)S(1)}, bf16[512,768]{1,0:T(8,128)(2,1)}, u32[]{:S(2)}) copy-start(bf16[512,768]{1,0:T(8,128)(2,1)} %copy-done.30) | copy-start | bytes 2359300
  207.8 8.2 %copy-start.26 = (bf16[512,768]{1,0:T(8,128)(2,1)S(1)}, bf16[512,768]{1,0:T(8,128)(2,1)}, u32[]{:S(2)}) copy-start(bf16[512,768]{1,0:T(8,128)(2,1)} %get-tuple-element.45) | copy-start | bytes 2359300
  207.8 5.2 %collective-permute-start.20 = (f32[16,768]{1,0:T(8,128)S(1)}, f32[16,768]{1,0:T(8,128)S(1)}, u32[]{:S(2)}, u32[]{:S(2)}) collective-permute-start(f32[16,768]{1,0:T(8,128)S(1)} %add.239), channel_id=1, source_target_pairs={{0,24},{4,28},{8,16},{12,20},{16,8},{20,12},{24,0},{28,4},{1,25},{... | collective-permute-start | bytes 147464 | tf_op jit(solution)/shard_map/ppermute | solution.py:157
  213.1 4.8 collective-permute-start.11
  215.4 6.9 %collective-permute-start.30 = (bf16[512,768]{1,0:T(8,128)(2,1)S(1)}, bf16[512,768]{1,0:T(8,128)(2,1)S(1)}, u32[]{:S(2)}, u32[]{:S(2)}) collective-permute-start(bf16[512,768]{1,0:T(8,128)(2,1)S(1)} %copy-done.31), channel_id=1, source_target_pairs={{0,1},{1,0},{2,3},{3,2},{4,5},{5,4},{6,7},{7,6},{8,9},{9,8},{10,11... | collective-permute-start | bytes 2359304 | tf_op jit(solution)/shard_map/ppermute | solution.py:154
  216.0 8.6 %collective-permute-start.37 = (bf16[512,768]{1,0:T(8,128)(2,1)S(1)}, bf16[512,768]{1,0:T(8,128)(2,1)S(1)}, u32[]{:S(2)}, u32[]{:S(2)}) collective-permute-start(bf16[512,768]{1,0:T(8,128)(2,1)S(1)} %copy-done.26), channel_id=1, source_target_pairs={{0,1},{1,0},{2,3},{3,2},{4,5},{5,4},{6,7},{7,6},{8,9},{9,8},{10,11... | collective-permute-start | bytes 2359304 | tf_op jit(solution)/shard_map/ppermute | solution.py:154
  217.9 7.4 %collective-permute-start.36 = (bf16[512,768]{1,0:T(8,128)(2,1)S(1)}, bf16[512,768]{1,0:T(8,128)(2,1)S(1)}, u32[]{:S(2)}, u32[]{:S(2)}) collective-permute-start(bf16[512,768]{1,0:T(8,128)(2,1)S(1)} %copy-done.9), channel_id=1, source_target_pairs={{0,1},{1,0},{2,3},{3,2},{4,5},{5,4},{6,7},{7,6},{8,9},{9,8},{10,11... | collective-permute-start | bytes 2359304 | tf_op jit(solution)/shard_map/ppermute | solution.py:154
  222.1 6.4 %collective-permute-start.29 = (bf16[512,768]{1,0:T(8,128)(2,1)S(1)}, bf16[512,768]{1,0:T(8,128)(2,1)S(1)}, u32[]{:S(2)}, u32[]{:S(2)}) collective-permute-start(bf16[512,768]{1,0:T(8,128)(2,1)S(1)} %copy-done.50), channel_id=1, source_target_pairs={{0,1},{1,0},{2,3},{3,2},{4,5},{5,4},{6,7},{7,6},{8,9},{9,8},{10,11... | collective-permute-start | bytes 2359304 | tf_op jit(solution)/shard_map/ppermute | solution.py:154
  222.3 51.2 %collective-permute-start.35 = (bf16[512,768]{1,0:T(8,128)(2,1)S(1)}, bf16[512,768]{1,0:T(8,128)(2,1)S(1)}, u32[]{:S(2)}, u32[]{:S(2)}) collective-permute-start(bf16[512,768]{1,0:T(8,128)(2,1)S(1)} %copy-done.48), channel_id=1, source_target_pairs={{0,1},{1,0},{2,3},{3,2},{4,5},{5,4},{6,7},{7,6},{8,9},{9,8},{10,11... | collective-permute-start | bytes 2359304 | tf_op jit(solution)/shard_map/ppermute | solution.py:154
  224.6 22.6 %collective-permute-start.12 = (bf16[576,768]{1,0:T(8,128)(2,1)S(1)}, bf16[576,768]{1,0:T(8,128)(2,1)S(1)}, u32[]{:S(2)}, u32[]{:S(2)}) collective-permute-start(bf16[576,768]{1,0:T(8,128)(2,1)S(1)} %add_convert_fusion.13), channel_id=1, source_target_pairs={{0,2},{1,3},{2,0},{3,1},{4,6},{5,7},{6,4},{7,5},{8,10},{9,11},{10,... | collective-permute-start | bytes 2654216 | tf_op jit(solution)/shard_map/ppermute | solution.py:154
  225.2 47.3 %collective-permute-start.31 = (bf16[768,768]{1,0:T(8,128)(2,1)S(1)}, bf16[768,768]{1,0:T(8,128)(2,1)S(1)}, u32[]{:S(2)}, u32[]{:S(2)}) collective-permute-start(bf16[768,768]{1,0:T(8,128)(2,1)S(1)} %add_convert_fusion.8), channel_id=1, source_target_pairs={{0,2},{1,3},{2,0},{3,1},{4,6},{5,7},{6,4},{7,5},{8,10},{9,11},{10,... | collective-permute-start | bytes 3538952 | tf_op jit(solution)/shard_map/ppermute | solution.py:154
  228.5 68.5 %collective-permute-start.38 = (bf16[768,768]{1,0:T(8,128)(2,1)S(1)}, bf16[768,768]{1,0:T(8,128)(2,1)S(1)}, u32[]{:S(2)}, u32[]{:S(2)}) collective-permute-start(bf16[768,768]{1,0:T(8,128)(2,1)S(1)} %add_convert_fusion.3), channel_id=1, source_target_pairs={{0,2},{1,3},{2,0},{3,1},{4,6},{5,7},{6,4},{7,5},{8,10},{9,11},{10,... | collective-permute-start | bytes 3538952 | tf_op jit(solution)/shard_map/ppermute | solution.py:154
  247.2 51.9 %collective-permute-start.22 = (bf16[512,768]{1,0:T(8,128)(2,1)S(1)}, bf16[512,768]{1,0:T(8,128)(2,1)S(1)}, u32[]{:S(2)}, u32[]{:S(2)}) collective-permute-start(bf16[512,768]{1,0:T(8,128)(2,1)S(1)} %copy-done), channel_id=1, source_target_pairs={{0,1},{1,0},{2,3},{3,2},{4,5},{5,4},{6,7},{7,6},{8,9},{9,8},{10,11... | collective-permute-start | bytes 2359304 | tf_op jit(solution)/shard_map/ppermute | solution.py:154
  247.4 27.5 %copy-start.2 = (f32[768,768]{1,0:T(8,128)S(1)}, f32[768,768]{1,0:T(8,128)}, u32[]{:S(2)}) copy-start(f32[768,768]{1,0:T(8,128)} %fusion.75) | copy-start | bytes 7077892
  272.5 27.9 %collective-permute-start.13 = (bf16[576,768]{1,0:T(8,128)(2,1)S(1)}, bf16[576,768]{1,0:T(8,128)(2,1)S(1)}, u32[]{:S(2)}, u32[]{:S(2)}) collective-permute-start(bf16[576,768]{1,0:T(8,128)(2,1)S(1)} %add_convert_fusion.12), channel_id=1, source_target_pairs={{0,4},{4,0},{8,12},{12,8},{16,20},{20,16},{24,28},{28,24},{1,5},{5... | collective-permute-start | bytes 2654216 | tf_op jit(solution)/shard_map/ppermute | solution.py:157
  273.4 23.5 %copy-start.22 = (bf16[512,192]{1,0:T(8,128)(2,1)S(1)}, bf16[512,192]{1,0:T(8,128)(2,1)}, u32[]{:S(2)}) copy-start(bf16[512,192]{1,0:T(8,128)(2,1)} %get-tuple-element.41.attended_ref) | copy-start | bytes 589828
  273.5 46.9 %collective-permute-start.32 = (bf16[768,768]{1,0:T(8,128)(2,1)S(1)}, bf16[768,768]{1,0:T(8,128)(2,1)S(1)}, u32[]{:S(2)}, u32[]{:S(2)}) collective-permute-start(bf16[768,768]{1,0:T(8,128)(2,1)S(1)} %add_convert_fusion.7), channel_id=1, source_target_pairs={{0,4},{4,0},{8,12},{12,8},{16,20},{20,16},{24,28},{28,24},{1,5},{5... | collective-permute-start | bytes 3538952 | tf_op jit(solution)/shard_map/ppermute | solution.py:157
  296.9 1.5 collective-permute-start.23
  298.5 47.2 %collective-permute-start.39 = (bf16[768,768]{1,0:T(8,128)(2,1)S(1)}, bf16[768,768]{1,0:T(8,128)(2,1)S(1)}, u32[]{:S(2)}, u32[]{:S(2)}) collective-permute-start(bf16[768,768]{1,0:T(8,128)(2,1)S(1)} %add_convert_fusion.2), channel_id=1, source_target_pairs={{0,4},{4,0},{8,12},{12,8},{16,20},{20,16},{24,28},{28,24},{1,5},{5... | collective-permute-start | bytes 3538952 | tf_op jit(solution)/shard_map/ppermute | solution.py:157
  299.8 22.2 %collective-permute-start.24 = (bf16[192,768]{1,0:T(8,128)(2,1)S(1)}, bf16[192,768]{1,0:T(8,128)(2,1)S(1)}, u32[]{:S(2)}, u32[]{:S(2)}) collective-permute-start(bf16[192,768]{1,0:T(8,128)(2,1)S(1)} %fusion.19), channel_id=1, source_target_pairs={{0,2},{1,3},{2,0},{3,1},{4,6},{5,7},{6,4},{7,5},{8,10},{9,11},{10,... | collective-permute-start | bytes 884744 | tf_op jit(solution)/shard_map/ppermute | solution.py:154
  300.6 21.4 %copy-start.15 = (f32[192,768]{1,0:T(8,128)S(1)}, f32[192,768]{1,0:T(8,128)}, u32[]{:S(2)}) copy-start(f32[192,768]{1,0:T(8,128)} %fusion.73) | copy-start | bytes 1769476
  300.7 50.1 %collective-permute-start.14 = (bf16[576,768]{1,0:T(8,128)(2,1)S(1)}, bf16[576,768]{1,0:T(8,128)(2,1)S(1)}, u32[]{:S(2)}, u32[]{:S(2)}) collective-permute-start(bf16[576,768]{1,0:T(8,128)(2,1)S(1)} %add_convert_fusion.11), channel_id=1, source_target_pairs={{0,8},{4,12},{8,0},{12,4},{16,24},{20,28},{24,16},{28,20},{1,9},{5... | collective-permute-start | bytes 2654216 | tf_op jit(solution)/shard_map/ppermute | solution.py:157
  320.7 30.7 %collective-permute-start.33 = (bf16[768,768]{1,0:T(8,128)(2,1)S(1)}, bf16[768,768]{1,0:T(8,128)(2,1)S(1)}, u32[]{:S(2)}, u32[]{:S(2)}) collective-permute-start(bf16[768,768]{1,0:T(8,128)(2,1)S(1)} %add_convert_fusion.6), channel_id=1, source_target_pairs={{0,8},{4,12},{8,0},{12,4},{16,24},{20,28},{24,16},{28,20},{1,9},{5... | collective-permute-start | bytes 3538952 | tf_op jit(solution)/shard_map/ppermute | solution.py:157
  323.3 26.1 %collective-permute-start.25 = (bf16[192,768]{1,0:T(8,128)(2,1)S(1)}, bf16[192,768]{1,0:T(8,128)(2,1)S(1)}, u32[]{:S(2)}, u32[]{:S(2)}) collective-permute-start(bf16[192,768]{1,0:T(8,128)(2,1)S(1)} %fusion.18), channel_id=1, source_target_pairs={{0,4},{4,0},{8,12},{12,8},{16,20},{20,16},{24,28},{28,24},{1,5},{5... | collective-permute-start | bytes 884744 | tf_op jit(solution)/shard_map/ppermute | solution.py:157
  346.0 35.4 %collective-permute-start.40 = (bf16[768,768]{1,0:T(8,128)(2,1)S(1)}, bf16[768,768]{1,0:T(8,128)(2,1)S(1)}, u32[]{:S(2)}, u32[]{:S(2)}) collective-permute-start(bf16[768,768]{1,0:T(8,128)(2,1)S(1)} %add_convert_fusion.1), channel_id=1, source_target_pairs={{0,8},{4,12},{8,0},{12,4},{16,24},{20,28},{24,16},{28,20},{1,9},{5... | collective-permute-start | bytes 3538952 | tf_op jit(solution)/shard_map/ppermute | solution.py:157
  349.4 31.8 %collective-permute-start.26 = (bf16[192,768]{1,0:T(8,128)(2,1)S(1)}, bf16[192,768]{1,0:T(8,128)(2,1)S(1)}, u32[]{:S(2)}, u32[]{:S(2)}) collective-permute-start(bf16[192,768]{1,0:T(8,128)(2,1)S(1)} %add_convert_fusion.17), channel_id=1, source_target_pairs={{0,8},{4,12},{8,0},{12,4},{16,24},{20,28},{24,16},{28,20},{1,9},{5... | collective-permute-start | bytes 884744 | tf_op jit(solution)/shard_map/ppermute | solution.py:157
  351.0 131.0 %collective-permute-start.15 = (bf16[576,768]{1,0:T(8,128)(2,1)S(1)}, bf16[576,768]{1,0:T(8,128)(2,1)S(1)}, u32[]{:S(2)}, u32[]{:S(2)}) collective-permute-start(bf16[576,768]{1,0:T(8,128)(2,1)S(1)} %add_convert_fusion.10), channel_id=1, source_target_pairs={{0,24},{4,28},{8,16},{12,20},{16,8},{20,12},{24,0},{28,4},{1,25},{... | collective-permute-start | bytes 2654216 | tf_op jit(solution)/shard_map/ppermute | solution.py:157
  351.7 131.6 %collective-permute-start.34 = (bf16[768,768]{1,0:T(8,128)(2,1)S(1)}, bf16[768,768]{1,0:T(8,128)(2,1)S(1)}, u32[]{:S(2)}, u32[]{:S(2)}) collective-permute-start(bf16[768,768]{1,0:T(8,128)(2,1)S(1)} %add_convert_fusion.5), channel_id=1, source_target_pairs={{0,24},{4,28},{8,16},{12,20},{16,8},{20,12},{24,0},{28,4},{1,25},{... | collective-permute-start | bytes 3538952 | tf_op jit(solution)/shard_map/ppermute | solution.py:157
  381.3 99.7 %collective-permute-start.27 = (bf16[192,768]{1,0:T(8,128)(2,1)S(1)}, bf16[192,768]{1,0:T(8,128)(2,1)S(1)}, u32[]{:S(2)}, u32[]{:S(2)}) collective-permute-start(bf16[192,768]{1,0:T(8,128)(2,1)S(1)} %add_convert_fusion.16), channel_id=1, source_target_pairs={{0,24},{4,28},{8,16},{12,20},{16,8},{20,12},{24,0},{28,4},{1,25},{... | collective-permute-start | bytes 884744 | tf_op jit(solution)/shard_map/ppermute | solution.py:157
  381.7 120.8 %collective-permute-start.41 = (bf16[768,768]{1,0:T(8,128)(2,1)S(1)}, bf16[768,768]{1,0:T(8,128)(2,1)S(1)}, u32[]{:S(2)}, u32[]{:S(2)}) collective-permute-start(bf16[768,768]{1,0:T(8,128)(2,1)S(1)} %add_convert_fusion), channel_id=1, source_target_pairs={{0,24},{4,28},{8,16},{12,20},{16,8},{20,12},{24,0},{28,4},{1,25},{... | collective-permute-start | bytes 3538952 | tf_op jit(solution)/shard_map/ppermute | solution.py:157
  (34 other events, 89.2 us)
